TPU v7x, 512 devices: a whole 4x8x8 slice. The times are simulated.
512 devices in a mesh: req: 128 (over y, z, core), tp: 4 (over x).
Axes of the slice: x: 4, y: 8, z: 8, core: 2. Of those that a mesh axis runs over, the one named last changes fastest.
Arguments:
- tokens: bfloat16 [16384, 1024], P('req'), may hold values from -6 to 6
- attn_heads: bfloat16 [16384, 1024], P('req', 'tp'), may hold values from -6 to 6
- out_proj: bfloat16 [1024, 1024], P('tp'), may hold values from -0.1875 to 0.1875
- norm_gain: float32 [1024], replicated, may hold values from 0.3 to 1.7
- w_gate: bfloat16 [32, 1024, 512], P(None, 'req', 'tp'), may hold values from -0.1875 to 0.1875
- w_up: bfloat16 [32, 1024, 512], P(None, 'req', 'tp'), may hold values from -0.1875 to 0.1875
- w_down: bfloat16 [32, 1024, 512], P(None, 'req', 'tp'), may hold values from -0.25 to 0.25
- routes: int32 [16384, 8], P('req'), may hold values from 0 to 31, all different within a row; in each aligned block of 32 rows (0 to 31, 32 to 63, ...) at most 12 rows name the same one
- gate_weights: float32 [16384, 8], P('req'), may hold values from 0.05 to 0.45
- cache_pages: bfloat16 [1024, 128, 8, 128], P('req', None, 'tp'), may hold values from -6 to 6
- page_dest: int32 [1024], P('req'), may hold values from 0 to 1023, as said below
Outputs:
- layer_output: bfloat16 [16384, 1024], P('req', 'tp')
- decode_cache: bfloat16 [1024, 128, 8, 128], P('req', None, 'tp')
Inputs may be any that keep to these rules, and one draw needn't show every extreme that they name: `routes`: within each aligned block of 32 rows no expert is named by more than 12 rows, and some block reaches 12. The page p of index r of req (p among its 8 pages) is sent to the index r + k modulo 128 for some k from 0 to 7, into its decode slot k: page_dest[p] = ((r + k) % 128) * 8 + k. The 8 pages of one index use each k once, so every decode slot gets one page.
All inputs are finite; a program needn't handle non-finite values.
Results may differ from a plain program's by a relative error of at most 0.012.
Values may be sent and summed in bfloat16 or wider, within the bound.
A program may use at most 64 MiB of HBM per device.

v0:
```python
import jax
import jax.numpy as jnp
import numpy as np
from jax import lax
from jax.sharding import PartitionSpec as P


def passed_along(value, axis, steps):
    count = lax.axis_size(axis)
    pairs = [(source, (source + steps) % count) for source in range(count)]
    return lax.ppermute(value, axis, pairs)


def on_device(
    tokens,
    attn_heads,
    out_proj,
    norm_gain,
    w_gate,
    w_up,
    w_down,
    routes,
    gate_weights,
    cache_pages,
    page_dest,
):
    req_count = lax.axis_size("req")
    tp_count = lax.axis_size("tp")
    tp_place = lax.axis_index("tp")
    tok_count, top_count = routes.shape
    experts = w_gate.shape[0]
    model_width = tokens.shape[1]
    quarter_width = model_width // tp_count
    partial_value = jnp.dot(attn_heads, out_proj, preferred_element_type=jnp.float32)
    attention = lax.psum(partial_value.astype(jnp.bfloat16), "tp").astype(jnp.float32)
    residual = tokens.astype(jnp.float32) + attention
    inverse = lax.rsqrt(jnp.mean(residual * residual, axis=1, keepdims=True) + 1e-05)
    normed = (residual * inverse * norm_gain).astype(jnp.bfloat16)
    resid_part = lax.dynamic_slice_in_dim(residual, tp_place * quarter_width, quarter_width, 1)
    local_experts = max(1, experts // req_count)
    expert_groups = experts // local_experts
    replicas = req_count // expert_groups
    block_rows = tok_count // replicas
    capacity = 3 * block_rows * top_count // (2 * experts)
    slot_total = req_count * local_experts * capacity
    expert_ids = jnp.arange(experts, dtype=jnp.int32)
    token_hits = jnp.sum((routes[:, :, None] == expert_ids).astype(jnp.int32), axis=1)
    blocked = token_hits.reshape(replicas, block_rows, experts)
    earlier = (jnp.cumsum(blocked, axis=1) - blocked).reshape(tok_count, experts)
    slot_rank = jnp.take_along_axis(earlier, routes, axis=1)
    row_ids = jnp.arange(tok_count, dtype=jnp.int32)[:, None]
    target = row_ids // block_rows * expert_groups + routes // local_experts
    slot_ids = (target * local_experts + routes % local_experts) * capacity + slot_rank
    flat_slots = slot_ids.reshape(-1)
    flat_rows = jnp.broadcast_to(row_ids, slot_ids.shape).reshape(-1)
    slot_token = jnp.zeros((slot_total,), jnp.int32).at[flat_slots].set(flat_rows)
    slot_live = jnp.zeros((slot_total,), jnp.bfloat16).at[flat_slots].set(1.0)
    owner_table = (
        np.arange(req_count)[:, None] % expert_groups * local_experts
        + np.arange(local_experts)[None, :]
    )
    outgoing = (w_gate[owner_table], w_up[owner_table], w_down[owner_table])
    gate_full, up_full, down_full = (
        lax.all_to_all(outgoing[0], "req", split_axis=0, concat_axis=2, tiled=True),
        lax.all_to_all(outgoing[1], "req", split_axis=0, concat_axis=2, tiled=True),
        lax.all_to_all(outgoing[2], "req", split_axis=0, concat_axis=2, tiled=True),
    )
    gate_full = gate_full[0]
    up_full = up_full[0]
    down_full = down_full[0]
    outbox = (normed[slot_token] * slot_live[:, None]).reshape(
        req_count, local_experts, capacity, model_width
    )
    arrived = lax.all_to_all(outbox, "req", split_axis=0, concat_axis=0, tiled=True)
    pre_gate = jnp.einsum("recd,edh->rech", arrived, gate_full, preferred_element_type=jnp.float32)
    pre_up = jnp.einsum("recd,edh->rech", arrived, up_full, preferred_element_type=jnp.float32)
    active = (jax.nn.silu(pre_gate) * pre_up).astype(jnp.bfloat16)
    pieces = jnp.einsum(
        "rech,edh->recd", active, down_full, preferred_element_type=jnp.float32
    ).astype(jnp.bfloat16)
    returned = lax.all_to_all(pieces, "req", split_axis=0, concat_axis=0, tiled=True)
    gathered = returned.reshape(slot_total, model_width)[slot_ids]
    combined = jnp.sum(gate_weights[:, :, None] * gathered.astype(jnp.float32), axis=1)
    mixture = lax.psum_scatter(
        combined.astype(jnp.bfloat16), "tp", scatter_dimension=1, tiled=True
    ).astype(jnp.float32)
    layer_output = (resid_part + mixture).astype(jnp.bfloat16)
    spread = cache_pages.shape[0]
    page_offsets = page_dest % spread
    page_order = (
        jnp.zeros((spread,), jnp.int32).at[page_offsets].set(jnp.arange(spread, dtype=jnp.int32))
    )
    ranked = cache_pages[page_order]
    arrived_pages = [ranked[0]]
    for offset in range(1, spread):
        arrived_pages.append(passed_along(ranked[offset], "req", offset))
    decode_cache = jnp.stack(arrived_pages)
    return (layer_output, decode_cache)


def solution(mesh):
    in_specs = (
        P("req", None),
        P("req", "tp"),
        P("tp", None),
        P(),
        P(None, "req", "tp"),
        P(None, "req", "tp"),
        P(None, "req", "tp"),
        P("req", None),
        P("req", None),
        P("req", None, "tp", None),
        P("req"),
    )
    out_specs = (P("req", "tp"), P("req", None, "tp", None))
    return jax.shard_map(
        on_device, mesh=mesh, in_specs=in_specs, out_specs=out_specs, check_vma=False
    )
```

profile of v0, /device:TPU:8, one launch (start us, length us, event | category | flops | bytes accessed | tf_op | source)
XLA Modules:
  0.0 437.8 jit_solution(17030307056659740838)
XLA Ops:
  7.2 2.1 convolution_convert_fusion
  9.3 0.7 compare_select_fusion.5
  10.0 0.6 scatter_custom_fusion.2
  10.6 0.7 pad_clamp_fusion.1
  11.3 2.2 gather_fusion.1
  13.5 17.4 %all-to-all-start.1 = ((bf16[128,1,8,128]{3,2,1,0:T(8,128)(2,1)}), bf16[128,1,8,128]{3,2,1,0:T(8,128)(2,1)S(1)}, u32[]{:S(2)}, u32[]{:S(2)}) async-start(bf16[128,1,8,128]{3,2,1,0:T(8,128)(2,1)} %bitcast.3), calls=%async_computation.1 | async-start | bytes 524288 | tf_op jit(solution)/shard_map/all_to_all | solution.py:64
  30.9 0.7 convert_reduce_fusion
  31.6 0.7 bitcast_or_fusion
  32.7 7.1 %gather_fusion.6 = s32[1024]{0:T(1024)S(1)} fusion(s32[128,32]{1,0:T(8,128)S(1)} %bitcast_subtract_fusion, s32[1024]{0:T(1024)S(1)} %reshape.217), kind=kCustom, calls=%fused_computation.6 | custom fusion | bytes 16384 | tf_op jit(solution)/shard_map/jit(take_along_axis)/gather | solution.py:50
  40.3 4.3 scatter_custom_fusion
  44.6 7.6 %scatter_custom_fusion.1 = bf16[1536]{0:T(1024)(128)(2,1)S(1)} fusion(s32[1024]{0:T(1024)S(1)} %bitcast.105, bf16[1024]{0:T(1024)(128)(2,1)S(1)} %broadcast.148, bf16[]{:T(256)} %constant.106.clone.1), kind=kCustom, calls=%fused_computation.73 | custom fusion | bytes 3074 | tf_op jit(solution)/shard_map/scatter | solution.py:57
  52.4 1.4 gather_fusion.3
  53.7 14.2 %all-reduce.2.cloned.1.call-done = bf16[128,1024]{1,0:T(8,128)(2,1)} async-done(((bf16[128,1024]{1,0:T(8,128)(2,1)}), bf16[128,1024]{1,0:T(8,128)(2,1)}) %all-reduce.2.cloned.1.call-update) | async-done | bytes 262160 | tf_op jit(solution)/shard_map/psum | solution.py:35
  67.9 1.1 convert_add_fusion
  69.0 14.2 %all-to-all-start.3 = ((bf16[128,1,8,128]{3,2,1,0:T(8,128)(2,1)}), bf16[128,1,8,128]{3,2,1,0:T(8,128)(2,1)S(1)}, u32[]{:S(2)}, u32[]{:S(2)}) async-start(bf16[128,1,8,128]{3,2,1,0:T(8,128)(2,1)} %bitcast.15), calls=%async_computation.3 | async-start | bytes 524288 | tf_op jit(solution)/shard_map/all_to_all | solution.py:65
  83.2 1.1 multiply_convert_fusion
  84.3 5.8 %gather_fusion.2 = bf16[1536,1024]{1,0:T(8,128)(2,1)} fusion(bf16[128,1024]{1,0:T(8,128)(2,1)S(1)} %multiply_convert_fusion, s32[2048]{0:T(1024)S(1)} %pad_clamp_fusion), kind=kCustom, calls=%fused_computation.2 | custom fusion | bytes 6297600 | tf_op jit(solution)/shard_map/gather | solution.py:71
  90.1 6.1 %gather.28 = bf16[128,1,12,1024]{3,2,0,1:T(8,128)(2,1)} reshape(bf16[1536,1024]{1,0:T(8,128)(2,1)} %gather_fusion.2) | data formatting | bytes 6291456 | tf_op jit(solution)/shard_map/gather | solution.py:71
  96.1 4.5 %multiply_bitcast_fusion = bf16[128,1,12,1024]{3,2,1,0:T(8,128)(2,1)} fusion(bf16[128,1,12,1024]{3,2,0,1:T(8,128)(2,1)} %gather.28, bf16[128,12]{1,0:T(8,128)(2,1)S(1)} %mul.78), kind=kLoop, calls=%fused_computation.12 | loop fusion | flops 1572864 | bytes 6294528 | tf_op jit(solution)/shard_map/mul | solution.py:71
  100.6 14.3 %all-to-all-start.2 = ((bf16[128,1,12,1024]{3,2,1,0:T(8,128)(2,1)}), bf16[128,1,12,1024]{3,2,1,0:T(8,128)(2,1)}, u32[]{:S(2)}, u32[]{:S(2)}) async-start(bf16[128,1,12,1024]{3,2,1,0:T(8,128)(2,1)} %multiply_bitcast_fusion), calls=%async_computation.2 | async-start | bytes 8388608 | tf_op jit(solution)/shard_map/all_to_all | solution.py:74
  115.0 1.4 gather_fusion
  116.3 95.0 %all-to-all-done.2 = bf16[128,1,12,1024]{3,2,1,0:T(8,128)(2,1)} async-done(((bf16[128,1,12,1024]{3,2,1,0:T(8,128)(2,1)}), bf16[128,1,12,1024]{3,2,1,0:T(8,128)(2,1)}, u32[]{:S(2)}, u32[]{:S(2)}) %all-to-all-start.2) | async-done | bytes 3145760 | tf_op jit(solution)/shard_map/all_to_all | solution.py:74
  211.3 16.5 %all-to-all-start = ((bf16[128,1,8,128]{3,2,1,0:T(8,128)(2,1)}), bf16[128,1,8,128]{3,2,1,0:T(8,128)(2,1)S(1)}, u32[]{:S(2)}, u32[]{:S(2)}) async-start(bf16[128,1,8,128]{3,2,1,0:T(8,128)(2,1)} %bitcast), calls=%async_computation | async-start | bytes 524288 | tf_op jit(solution)/shard_map/all_to_all | solution.py:66
  227.8 5.8 %fusion.7 = f32[128,1,12,128]{0,3,2,1:T(8,128)S(1)} fusion(bf16[128,1,12,1024]{3,2,1,0:T(8,128)(2,1)} %all-to-all-done.2, bf16[128,1,8,128]{3,2,1,0:T(8,128)(2,1)S(1)} %all-to-all-done.1), kind=kOutput, calls=%fused_computation.20 | convolution fusion | flops 402653184 | bytes 4194304 | tf_op jit(solution)/shard_map/recd,edh->rech/dot_general | solution.py:75
  233.6 8.9 %all-to-all-done = bf16[128,1,8,128]{3,2,1,0:T(8,128)(2,1)S(1)} async-done(((bf16[128,1,8,128]{3,2,1,0:T(8,128)(2,1)}), bf16[128,1,8,128]{3,2,1,0:T(8,128)(2,1)S(1)}, u32[]{:S(2)}, u32[]{:S(2)}) %all-to-all-start) | async-done | bytes 262176 | tf_op jit(solution)/shard_map/all_to_all | solution.py:66
  242.5 8.4 %convert_bitcast_fusion = bf16[128,1,12,1024]{0,3,2,1:T(8,128)(2,1)} fusion(bf16[128,1,12,1024]{3,2,1,0:T(8,128)(2,1)} %all-to-all-done.2, f32[128,1,12,128]{0,3,2,1:T(8,128)S(1)} %fusion.7, bf16[128,1,8,128]{3,2,1,0:T(8,128)(2,1)S(1)} %all-to-all-done.3, bf16[128,1,8,128]{3,2,1,0:T(8,128)(2,1)S(1)} %all-to-all-done), kind=kOutput, calls=%fused_computation.17 | convolution fusion | flops 808058880 | bytes 7602176 | tf_op jit(solution)/shard_map/rech,edh->recd/dot_general | solution.py:78
  250.9 6.5 %copy.82 = bf16[128,1,12,1024]{3,2,1,0:T(8,128)(2,1)} copy(bf16[128,1,12,1024]{0,3,2,1:T(8,128)(2,1)} %convert_bitcast_fusion) | data formatting | bytes 6291456 | tf_op jit(solution)/shard_map/convert_element_type | solution.py:80
  257.4 7.8 %all-to-all-start.4 = ((bf16[128,1,12,1024]{3,2,1,0:T(8,128)(2,1)}), bf16[128,1,12,1024]{3,2,1,0:T(8,128)(2,1)}, u32[]{:S(2)}, u32[]{:S(2)}) async-start(bf16[128,1,12,1024]{3,2,1,0:T(8,128)(2,1)} %copy.82), calls=%async_computation.4 | async-start | bytes 8388608 | tf_op jit(solution)/shard_map/all_to_all | solution.py:81
  265.2 0.3 reduce-scatter.2.cloned.1.call-start
  265.5 1.6 gather_fusion.5
  267.1 0.4 slice_bitcast_fusion
  267.5 2.1 collective-permute-start
  269.6 3.4 collective-permute-start.1
  272.9 4.2 collective-permute-start.2
  277.1 4.6 %collective-permute-start.3 = (bf16[128,2,128]{2,1,0:T(2,128)(2,1)S(1)}, bf16[128,2,128]{2,1,0:T(2,128)(2,1)S(1)}, u32[]{:S(2)}, u32[]{:S(2)}) collective-permute-start(bf16[128,2,128]{2,1,0:T(2,128)(2,1)S(1)} %get-tuple-element.7), channel_id=1, source_target_pairs={{0,16},{4,20},{8,24},{12,28},{16,32},{20,36},{24,40},{28,44},{32,4... | collective-permute-start | bytes 196616 | tf_op jit(solution)/shard_map/ppermute | solution.py:11
  281.7 2.1 collective-permute-start.4
  284.1 74.4 %collective-permute-done = bf16[128,2,128]{2,1,0:T(2,128)(2,1)S(1)} collective-permute-done((bf16[128,2,128]{2,1,0:T(2,128)(2,1)S(1)}, bf16[128,2,128]{2,1,0:T(2,128)(2,1)S(1)}, u32[]{:S(2)}, u32[]{:S(2)}) %collective-permute-start) | collective-permute-done | bytes 65568 | tf_op jit(solution)/shard_map/ppermute | solution.py:11
  358.5 5.6 %collective-permute-start.5 = (bf16[128,2,128]{2,1,0:T(2,128)(2,1)S(1)}, bf16[128,2,128]{2,1,0:T(2,128)(2,1)S(1)}, u32[]{:S(2)}, u32[]{:S(2)}) collective-permute-start(bf16[128,2,128]{2,1,0:T(2,128)(2,1)S(1)} %get-tuple-element.5), channel_id=1, source_target_pairs={{0,24},{4,28},{8,32},{12,36},{16,40},{20,44},{24,48},{28,52},{32,5... | collective-permute-start | bytes 196616 | tf_op jit(solution)/shard_map/ppermute | solution.py:11
  364.2 22.5 %collective-permute-start.6 = (bf16[128,2,128]{2,1,0:T(2,128)(2,1)S(1)}, bf16[128,2,128]{2,1,0:T(2,128)(2,1)}, u32[]{:S(2)}, u32[]{:S(2)}) collective-permute-start(bf16[128,2,128]{2,1,0:T(2,128)(2,1)S(1)} %get-tuple-element.4), channel_id=1, source_target_pairs={{0,28},{4,32},{8,36},{12,40},{16,44},{20,48},{24,52},{28,56},{32,6... | collective-permute-start | bytes 196616 | tf_op jit(solution)/shard_map/ppermute | solution.py:11
  386.9 0.8 copy-done.5
  387.7 6.1 %reshape.168 = bf16[1536,1024]{1,0:T(8,128)(2,1)} reshape(bf16[128,1,12,1024]{3,2,1,0:T(8,128)(2,1)} %all-to-all-done.4) | data formatting | bytes 6291456 | tf_op jit(solution)/shard_map/reshape | solution.py:82
  393.8 7.3 %gather_fusion.4 = bf16[1024,1024]{1,0:T(8,128)(2,1)S(1)} fusion(bf16[1536,1024]{1,0:T(8,128)(2,1)} %reshape.168, s32[1024]{0:T(1024)S(1)} %broadcast_clamp_fusion), kind=kCustom, calls=%fused_computation.4 | custom fusion | bytes 4198400 | tf_op jit(solution)/shard_map/gather | solution.py:82
  401.1 2.0 fusion
  403.1 0.7 bitcast_dynamic-update-slice_fusion.2
  403.8 0.7 bitcast_dynamic-update-slice_fusion.1
  404.5 1.5 bitcast_dynamic-update-slice_fusion
  406.0 23.4 %reduce-scatter.2.cloned.1.call-done = bf16[128,256]{1,0:T(8,128)(2,1)} async-done(((bf16[128,1024]{1,0:T(8,128)(2,1)}), bf16[128,256]{1,0:T(8,128)(2,1)}) %reduce-scatter.2.cloned.1.call-update) | async-done | bytes 65552 | tf_op jit(solution)/shard_map/reduce_scatter | solution.py:84
  429.5 1.5 add_convert_fusion
  (56 shorter events, 1.7 us)
Async XLA Ops:
  7.2 258.3 %copy-start = (bf16[8,128,2,128]{3,2,1,0:T(2,128)(2,1)S(1)}, bf16[8,128,2,128]{3,2,1,0:T(2,128)(2,1)}, u32[]{:S(2)}) copy-start(bf16[8,128,2,128]{3,2,1,0:T(2,128)(2,1)} %param.24) | copy-start | bytes 1572868
  7.2 60.7 %all-reduce.2.cloned.1.call-start = ((), (), s32[]{:S(2)}) async-start(), calls=%async_computation.6 | async-start | bytes 524288 | tf_op jit(solution)/shard_map/psum | solution.py:35
  13.5 55.5 %all-to-all-start.1 = ((bf16[128,1,8,128]{3,2,1,0:T(8,128)(2,1)}), bf16[128,1,8,128]{3,2,1,0:T(8,128)(2,1)S(1)}, u32[]{:S(2)}, u32[]{:S(2)}) async-start(bf16[128,1,8,128]{3,2,1,0:T(8,128)(2,1)} %bitcast.3), calls=%async_computation.1 | async-start | bytes 524288 | tf_op jit(solution)/shard_map/all_to_all | solution.py:64
  32.6 7.3 %copy-start.4 = (s32[128,8]{0,1:T(8,128)S(1)}, s32[128,8]{0,1:T(8,128)}, u32[]{:S(2)}) copy-start(s32[128,8]{0,1:T(8,128)} %param.22) | copy-start | bytes 12292
  32.7 19.7 %copy-start.1 = (bf16[32,8,128]{2,1,0:T(8,128)(2,1)S(1)}, bf16[32,8,128]{2,1,0:T(8,128)(2,1)}, u32[]{:S(2)}) copy-start(bf16[32,8,128]{2,1,0:T(8,128)(2,1)} %param.20) | copy-start | bytes 196612
  32.7 35.2 %copy-start.3 = (bf16[128,1024]{1,0:T(8,128)(2,1)S(1)}, bf16[128,1024]{1,0:T(8,128)(2,1)}, u32[]{:S(2)}) copy-start(bf16[128,1024]{1,0:T(8,128)(2,1)} %param.15) | copy-start | bytes 786436
  32.7 50.5 %copy-start.6 = (f32[1024]{0:T(1024)S(1)}, f32[1024]{0:T(1024)}, u32[]{:S(2)}) copy-start(f32[1024]{0:T(1024)} %param.18) | copy-start | bytes 12292
  69.0 31.6 %all-to-all-start.3 = ((bf16[128,1,8,128]{3,2,1,0:T(8,128)(2,1)}), bf16[128,1,8,128]{3,2,1,0:T(8,128)(2,1)S(1)}, u32[]{:S(2)}, u32[]{:S(2)}) async-start(bf16[128,1,8,128]{3,2,1,0:T(8,128)(2,1)} %bitcast.15), calls=%async_computation.3 | async-start | bytes 524288 | tf_op jit(solution)/shard_map/all_to_all | solution.py:65
  100.6 14.3 %copy-start.2 = (bf16[32,8,128]{2,1,0:T(8,128)(2,1)S(1)}, bf16[32,8,128]{2,1,0:T(8,128)(2,1)}, u32[]{:S(2)}) copy-start(bf16[32,8,128]{2,1,0:T(8,128)(2,1)} %param.21) | copy-start | bytes 196612
  100.6 110.7 %all-to-all-start.2 = ((bf16[128,1,12,1024]{3,2,1,0:T(8,128)(2,1)}), bf16[128,1,12,1024]{3,2,1,0:T(8,128)(2,1)}, u32[]{:S(2)}, u32[]{:S(2)}) async-start(bf16[128,1,12,1024]{3,2,1,0:T(8,128)(2,1)} %multiply_bitcast_fusion), calls=%async_computation.2 | async-start | bytes 8388608 | tf_op jit(solution)/shard_map/all_to_all | solution.py:74
  211.3 31.2 %all-to-all-start = ((bf16[128,1,8,128]{3,2,1,0:T(8,128)(2,1)}), bf16[128,1,8,128]{3,2,1,0:T(8,128)(2,1)S(1)}, u32[]{:S(2)}, u32[]{:S(2)}) async-start(bf16[128,1,8,128]{3,2,1,0:T(8,128)(2,1)} %bitcast), calls=%async_computation | async-start | bytes 524288 | tf_op jit(solution)/shard_map/all_to_all | solution.py:66
  257.4 26.6 %copy-start.7 = (f32[128,8]{0,1:T(8,128)S(1)}, f32[128,8]{0,1:T(8,128)}, u32[]{:S(2)}) copy-start(f32[128,8]{0,1:T(8,128)} %param.23) | copy-start | bytes 12292
  257.4 129.5 %all-to-all-start.4 = ((bf16[128,1,12,1024]{3,2,1,0:T(8,128)(2,1)}), bf16[128,1,12,1024]{3,2,1,0:T(8,128)(2,1)}, u32[]{:S(2)}, u32[]{:S(2)}) async-start(bf16[128,1,12,1024]{3,2,1,0:T(8,128)(2,1)} %copy.82), calls=%async_computation.4 | async-start | bytes 8388608 | tf_op jit(solution)/shard_map/all_to_all | solution.py:81
  265.2 164.2 %reduce-scatter.2.cloned.1.call-start = ((), (), s32[]{:S(2)}) async-start(), calls=%async_computation.7 | async-start | bytes 327680 | tf_op jit(solution)/shard_map/reduce_scatter | solution.py:84
  267.5 91.0 %collective-permute-start = (bf16[128,2,128]{2,1,0:T(2,128)(2,1)S(1)}, bf16[128,2,128]{2,1,0:T(2,128)(2,1)S(1)}, u32[]{:S(2)}, u32[]{:S(2)}) collective-permute-start(bf16[128,2,128]{2,1,0:T(2,128)(2,1)S(1)} %get-tuple-element.10), channel_id=1, source_target_pairs={{0,4},{4,8},{8,12},{12,16},{16,20},{20,24},{24,28},{28,32},{32,36}... | collective-permute-start | bytes 196616 | tf_op jit(solution)/shard_map/ppermute | solution.py:11
  269.6 94.6 %collective-permute-start.1 = (bf16[128,2,128]{2,1,0:T(2,128)(2,1)S(1)}, bf16[128,2,128]{2,1,0:T(2,128)(2,1)S(1)}, u32[]{:S(2)}, u32[]{:S(2)}) collective-permute-start(bf16[128,2,128]{2,1,0:T(2,128)(2,1)S(1)} %get-tuple-element.9), channel_id=1, source_target_pairs={{0,8},{4,12},{8,16},{12,20},{16,24},{20,28},{24,32},{28,36},{32,40... | collective-permute-start | bytes 196616 | tf_op jit(solution)/shard_map/ppermute | solution.py:11
  272.9 113.8 %collective-permute-start.2 = (bf16[128,2,128]{2,1,0:T(2,128)(2,1)S(1)}, bf16[128,2,128]{2,1,0:T(2,128)(2,1)S(1)}, u32[]{:S(2)}, u32[]{:S(2)}) collective-permute-start(bf16[128,2,128]{2,1,0:T(2,128)(2,1)S(1)} %get-tuple-element.8), channel_id=1, source_target_pairs={{0,12},{4,16},{8,20},{12,24},{16,28},{20,32},{24,36},{28,40},{32,4... | collective-permute-start | bytes 196616 | tf_op jit(solution)/shard_map/ppermute | solution.py:11
  277.1 109.7 %collective-permute-start.3 = (bf16[128,2,128]{2,1,0:T(2,128)(2,1)S(1)}, bf16[128,2,128]{2,1,0:T(2,128)(2,1)S(1)}, u32[]{:S(2)}, u32[]{:S(2)}) collective-permute-start(bf16[128,2,128]{2,1,0:T(2,128)(2,1)S(1)} %get-tuple-element.7), channel_id=1, source_target_pairs={{0,16},{4,20},{8,24},{12,28},{16,32},{20,36},{24,40},{28,44},{32,4... | collective-permute-start | bytes 196616 | tf_op jit(solution)/shard_map/ppermute | solution.py:11
  281.7 121.4 %collective-permute-start.4 = (bf16[128,2,128]{2,1,0:T(2,128)(2,1)S(1)}, bf16[128,2,128]{2,1,0:T(2,128)(2,1)S(1)}, u32[]{:S(2)}, u32[]{:S(2)}) collective-permute-start(bf16[128,2,128]{2,1,0:T(2,128)(2,1)S(1)} %get-tuple-element.6), channel_id=1, source_target_pairs={{0,20},{4,24},{8,28},{12,32},{16,36},{20,40},{24,44},{28,48},{32,5... | collective-permute-start | bytes 196616 | tf_op jit(solution)/shard_map/ppermute | solution.py:11
  358.5 45.3 %collective-permute-start.5 = (bf16[128,2,128]{2,1,0:T(2,128)(2,1)S(1)}, bf16[128,2,128]{2,1,0:T(2,128)(2,1)S(1)}, u32[]{:S(2)}, u32[]{:S(2)}) collective-permute-start(bf16[128,2,128]{2,1,0:T(2,128)(2,1)S(1)} %get-tuple-element.5), channel_id=1, source_target_pairs={{0,24},{4,28},{8,32},{12,36},{16,40},{20,44},{24,48},{28,52},{32,5... | collective-permute-start | bytes 196616 | tf_op jit(solution)/shard_map/ppermute | solution.py:11
  364.2 40.3 %collective-permute-start.6 = (bf16[128,2,128]{2,1,0:T(2,128)(2,1)S(1)}, bf16[128,2,128]{2,1,0:T(2,128)(2,1)}, u32[]{:S(2)}, u32[]{:S(2)}) collective-permute-start(bf16[128,2,128]{2,1,0:T(2,128)(2,1)S(1)} %get-tuple-element.4), channel_id=1, source_target_pairs={{0,28},{4,32},{8,36},{12,40},{16,44},{20,48},{24,52},{28,56},{32,6... | collective-permute-start | bytes 196616 | tf_op jit(solution)/shard_map/ppermute | solution.py:11
  386.9 0.8 copy-start.5
Sparse Core Ops, SparseCore 0:
  10.9 56.9 all-reduce.1
  403.2 26.1 reduce-scatter.1
where the time goes:
time: 439 us; the launch traced here: 438 us
  waiting for transfers between devices  216 us (49%)
  starting transfers between devices  115 us (26%)
  local copies, waits for them, and re-layouts  63.4 us (14%)
  matrix products  16.2 us (4%)
  between operations  14.4 us (3%)
  other arithmetic  13 us (3%)
    all_to_all x1, waiting for transfers between devices, on_device(): lax.all_to_all(outbox, 'req', split_axis=0, concat_axis=0, tiled=True)  95 us
    ppermute x7, waiting for transfers between devices, passed_along(): return lax.ppermute(value, axis, pairs)  74.4 us
    ppermute x7, starting transfers between devices, passed_along(): return lax.ppermute(value, axis, pairs)  44.4 us
    reduce_scatter x1, waiting for transfers between devices, on_device(): lax.psum_scatter(combined.astype(jnp.bfloat16), 'tp', scatter_dimension=1...  23.4 us
    all_to_all x1, starting transfers between devices, on_device(): lax.all_to_all(outgoing[0], 'req', split_axis=0, concat_axis=2, tiled=True)  17.4 us
    all_to_all x1, starting transfers between devices, on_device(): lax.all_to_all(outgoing[2], 'req', split_axis=0, concat_axis=2, tiled=True)  16.5 us
    all_to_all x1, starting transfers between devices, on_device(): lax.all_to_all(outbox, 'req', split_axis=0, concat_axis=0, tiled=True)  14.3 us
    all_to_all x1, starting transfers between devices, on_device(): lax.all_to_all(outgoing[1], 'req', split_axis=0, concat_axis=2, tiled=True)  14.2 us
  transfers between devices with their start and end apart: 14, of which 5 were waited for; matrix products, arithmetic and copies ran while one was open for 17% of the time, Pallas kernels for 0%

commit v1 on v0

--- a/solution.py
+++ b/solution.py
@@ -32,7 +32,9 @@
     model_width = tokens.shape[1]
     quarter_width = model_width // tp_count
     partial_value = jnp.dot(attn_heads, out_proj, preferred_element_type=jnp.float32)
-    attention = lax.psum(partial_value.astype(jnp.bfloat16), "tp").astype(jnp.float32)
+    attention = jnp.sum(lax.all_gather(partial_value.astype(jnp.bfloat16), "tp"), axis=0).astype(
+        jnp.float32
+    )
     residual = tokens.astype(jnp.float32) + attention
     inverse = lax.rsqrt(jnp.mean(residual * residual, axis=1, keepdims=True) + 1e-05)
     normed = (residual * inverse * norm_gain).astype(jnp.bfloat16)

time: 439 us -> 425 us (0.968)
  waiting for transfers between devices: 216 us -> 202 us
    psum x1 -> x0, waiting for transfers between devices: 14.2 us -> none  [on_device(): lax.psum(partial_value.astype(jnp.bfloat16), 'tp').astype(jnp.float32)]
  transfers between devices with their start and end apart: 14 -> 14, of which waited for: 5 -> 4; matrix products, arithmetic and copies ran while one was open for 17% -> 17% of each run, Pallas kernels for 0% -> 0%
where the time goes in v1:
time: 425 us; the launch traced here: 424 us
  waiting for transfers between devices  202 us (48%)
  starting transfers between devices  114 us (27%)
  local copies, waits for them, and re-layouts  63.4 us (15%)
  matrix products  17.3 us (4%)
  between operations  14.4 us (3%)
  other arithmetic  12.6 us (3%)
    all_to_all x1, waiting for transfers between devices, on_device(): lax.all_to_all(outbox, 'req', split_axis=0, concat_axis=0, tiled=True)  95 us
    ppermute x7, waiting for transfers between devices, passed_along(): return lax.ppermute(value, axis, pairs)  74.4 us
    ppermute x7, starting transfers between devices, passed_along(): return lax.ppermute(value, axis, pairs)  44.4 us
    reduce_scatter x1, waiting for transfers between devices, on_device(): lax.psum_scatter(combined.astype(jnp.bfloat16), 'tp', scatter_dimension=1...  24.3 us
    all_to_all x1, starting transfers between devices, on_device(): lax.all_to_all(outgoing[0], 'req', split_axis=0, concat_axis=2, tiled=True)  17.4 us
    all_to_all x1, starting transfers between devices, on_device(): lax.all_to_all(outgoing[2], 'req', split_axis=0, concat_axis=2, tiled=True)  16.5 us
    all_to_all x1, starting transfers between devices, on_device(): lax.all_to_all(outbox, 'req', split_axis=0, concat_axis=0, tiled=True)  14.3 us
    all_to_all x1, starting transfers between devices, on_device(): lax.all_to_all(outgoing[1], 'req', split_axis=0, concat_axis=2, tiled=True)  13.7 us
  transfers between devices with their start and end apart: 14, of which 4 were waited for; matrix products, arithmetic and copies ran while one was open for 17% of the time, Pallas kernels for 0%

profile of v1, /device:TPU:8, one launch (start us, length us, event | category | flops | bytes accessed | tf_op | source)
XLA Modules:
  0.0 423.8 jit_solution(14566156517347515180)
XLA Ops:
  7.2 2.1 convolution_convert_fusion
  9.3 0.7 compare_select_fusion.5
  10.0 0.6 scatter_custom_fusion.2
  10.6 0.7 pad_clamp_fusion.1
  11.3 2.2 gather_fusion.1
  13.5 17.4 %all-to-all-start.1 = ((bf16[128,1,8,128]{3,2,1,0:T(8,128)(2,1)}), bf16[128,1,8,128]{3,2,1,0:T(8,128)(2,1)S(1)}, u32[]{:S(2)}, u32[]{:S(2)}) async-start(bf16[128,1,8,128]{3,2,1,0:T(8,128)(2,1)} %bitcast.4), calls=%async_computation.1 | async-start | bytes 524288 | tf_op jit(solution)/shard_map/all_to_all | solution.py:66
  30.8 0.7 convert_reduce_fusion
  31.7 0.7 bitcast_or_fusion
  32.7 7.1 %gather_fusion.6 = s32[1024]{0:T(1024)S(1)} fusion(s32[128,32]{1,0:T(8,128)S(1)} %bitcast_subtract_fusion, s32[1024]{0:T(1024)S(1)} %reshape.217), kind=kCustom, calls=%fused_computation.6 | custom fusion | bytes 16384 | tf_op jit(solution)/shard_map/jit(take_along_axis)/gather | solution.py:52
  40.3 4.3 %scatter_custom_fusion = s32[1536]{0:T(1024)S(1)} fusion(s32[1024]{0:T(1024)S(1)} %bitcast.106, s32[1024]{0:T(1024)S(1)} %reshape.227, s32[]{:T(128)} %constant.92.clone.1), kind=kCustom, calls=%fused_computation.66 | custom fusion | bytes 6148 | tf_op jit(solution)/shard_map/scatter | solution.py:58
  44.6 7.6 %scatter_custom_fusion.1 = bf16[1536]{0:T(1024)(128)(2,1)S(1)} fusion(s32[1024]{0:T(1024)S(1)} %bitcast.107, bf16[1024]{0:T(1024)(128)(2,1)S(1)} %broadcast.148, bf16[]{:T(256)} %constant.91.clone.1), kind=kCustom, calls=%fused_computation.73 | custom fusion | bytes 3074 | tf_op jit(solution)/shard_map/scatter | solution.py:59
  52.2 0.1 mul.78
  52.4 1.4 gather_fusion.3
  53.7 1.4 reduce_sum.39
  55.2 0.2 convert_add_fusion
  55.4 13.7 %all-to-all-start.3 = ((bf16[128,1,8,128]{3,2,1,0:T(8,128)(2,1)}), bf16[128,1,8,128]{3,2,1,0:T(8,128)(2,1)S(1)}, u32[]{:S(2)}, u32[]{:S(2)}) async-start(bf16[128,1,8,128]{3,2,1,0:T(8,128)(2,1)} %bitcast.16), calls=%async_computation.3 | async-start | bytes 524288 | tf_op jit(solution)/shard_map/all_to_all | solution.py:67
  69.2 5.8 %gather_fusion.2 = bf16[1536,1024]{1,0:T(8,128)(2,1)} fusion(bf16[128,1024]{1,0:T(8,128)(2,1)S(1)} %multiply_convert_fusion, s32[2048]{0:T(1024)S(1)} %pad_clamp_fusion), kind=kCustom, calls=%fused_computation.2 | custom fusion | bytes 6297600 | tf_op jit(solution)/shard_map/gather | solution.py:73
  75.0 6.1 %gather.28 = bf16[128,1,12,1024]{3,2,0,1:T(8,128)(2,1)} reshape(bf16[1536,1024]{1,0:T(8,128)(2,1)} %gather_fusion.2) | data formatting | bytes 6291456 | tf_op jit(solution)/shard_map/gather | solution.py:73
  81.1 4.5 %multiply_bitcast_fusion = bf16[128,1,12,1024]{3,2,1,0:T(8,128)(2,1)} fusion(bf16[128,1,12,1024]{3,2,0,1:T(8,128)(2,1)} %gather.28, bf16[128,12]{1,0:T(8,128)(2,1)S(1)} %mul.78), kind=kLoop, calls=%fused_computation.12 | loop fusion | flops 1572864 | bytes 6294528 | tf_op jit(solution)/shard_map/mul | solution.py:73
  85.6 14.3 %all-to-all-start.2 = ((bf16[128,1,12,1024]{3,2,1,0:T(8,128)(2,1)}), bf16[128,1,12,1024]{3,2,1,0:T(8,128)(2,1)}, u32[]{:S(2)}, u32[]{:S(2)}) async-start(bf16[128,1,12,1024]{3,2,1,0:T(8,128)(2,1)} %multiply_bitcast_fusion), calls=%async_computation.2 | async-start | bytes 8388608 | tf_op jit(solution)/shard_map/all_to_all | solution.py:76
  99.9 1.4 gather_fusion
  101.3 95.0 %all-to-all-done.2 = bf16[128,1,12,1024]{3,2,1,0:T(8,128)(2,1)} async-done(((bf16[128,1,12,1024]{3,2,1,0:T(8,128)(2,1)}), bf16[128,1,12,1024]{3,2,1,0:T(8,128)(2,1)}, u32[]{:S(2)}, u32[]{:S(2)}) %all-to-all-start.2) | async-done | bytes 3145760 | tf_op jit(solution)/shard_map/all_to_all | solution.py:76
  196.3 16.5 %all-to-all-start = ((bf16[128,1,8,128]{3,2,1,0:T(8,128)(2,1)}), bf16[128,1,8,128]{3,2,1,0:T(8,128)(2,1)S(1)}, u32[]{:S(2)}, u32[]{:S(2)}) async-start(bf16[128,1,8,128]{3,2,1,0:T(8,128)(2,1)} %bitcast.1), calls=%async_computation | async-start | bytes 524288 | tf_op jit(solution)/shard_map/all_to_all | solution.py:68
  212.7 6.7 %fusion.7 = f32[128,1,12,128]{0,3,2,1:T(8,128)} fusion(bf16[128,1,12,1024]{3,2,1,0:T(8,128)(2,1)} %all-to-all-done.2, bf16[128,1,8,128]{3,2,1,0:T(8,128)(2,1)S(1)} %all-to-all-done.1), kind=kOutput, calls=%fused_computation.20 | convolution fusion | flops 402653184 | bytes 4194304 | tf_op jit(solution)/shard_map/recd,edh->rech/dot_general | solution.py:77
  219.4 8.1 %all-to-all-done = bf16[128,1,8,128]{3,2,1,0:T(8,128)(2,1)S(1)} async-done(((bf16[128,1,8,128]{3,2,1,0:T(8,128)(2,1)}), bf16[128,1,8,128]{3,2,1,0:T(8,128)(2,1)S(1)}, u32[]{:S(2)}, u32[]{:S(2)}) %all-to-all-start) | async-done | bytes 262176 | tf_op jit(solution)/shard_map/all_to_all | solution.py:68
  227.5 8.6 %convert_bitcast_fusion = bf16[128,1,12,1024]{0,3,2,1:T(8,128)(2,1)} fusion(bf16[128,1,12,1024]{3,2,1,0:T(8,128)(2,1)} %all-to-all-done.2, f32[128,1,12,128]{0,3,2,1:T(8,128)} %fusion.7, bf16[128,1,8,128]{3,2,1,0:T(8,128)(2,1)S(1)} %all-to-all-done.3, bf16[128,1,8,128]{3,2,1,0:T(8,128)(2,1)S(1)} %all-to-all-done), kind=kOutput, calls=%fused_computation.17 | convolution fusion | flops 808058880 | bytes 7602176 | tf_op jit(solution)/shard_map/rech,edh->recd/dot_general | solution.py:80
  236.1 6.5 %copy.82 = bf16[128,1,12,1024]{3,2,1,0:T(8,128)(2,1)} copy(bf16[128,1,12,1024]{0,3,2,1:T(8,128)(2,1)} %convert_bitcast_fusion) | data formatting | bytes 6291456 | tf_op jit(solution)/shard_map/convert_element_type | solution.py:82
  242.6 7.8 %all-to-all-start.4 = ((bf16[128,1,12,1024]{3,2,1,0:T(8,128)(2,1)}), bf16[128,1,12,1024]{3,2,1,0:T(8,128)(2,1)}, u32[]{:S(2)}, u32[]{:S(2)}) async-start(bf16[128,1,12,1024]{3,2,1,0:T(8,128)(2,1)} %copy.82), calls=%async_computation.4 | async-start | bytes 8388608 | tf_op jit(solution)/shard_map/all_to_all | solution.py:83
  250.4 0.3 reduce-scatter.2.cloned.1.call-start
  250.7 1.6 gather_fusion.5
  252.3 0.4 slice_bitcast_fusion
  252.7 2.1 collective-permute-start
  254.7 3.4 collective-permute-start.1
  258.1 4.2 collective-permute-start.2
  262.3 4.6 %collective-permute-start.3 = (bf16[128,2,128]{2,1,0:T(2,128)(2,1)S(1)}, bf16[128,2,128]{2,1,0:T(2,128)(2,1)S(1)}, u32[]{:S(2)}, u32[]{:S(2)}) collective-permute-start(bf16[128,2,128]{2,1,0:T(2,128)(2,1)S(1)} %get-tuple-element.7), channel_id=1, source_target_pairs={{0,16},{4,20},{8,24},{12,28},{16,32},{20,36},{24,40},{28,44},{32,4... | collective-permute-start | bytes 196616 | tf_op jit(solution)/shard_map/ppermute | solution.py:11
  266.9 2.1 collective-permute-start.4
  269.3 74.4 %collective-permute-done = bf16[128,2,128]{2,1,0:T(2,128)(2,1)S(1)} collective-permute-done((bf16[128,2,128]{2,1,0:T(2,128)(2,1)S(1)}, bf16[128,2,128]{2,1,0:T(2,128)(2,1)S(1)}, u32[]{:S(2)}, u32[]{:S(2)}) %collective-permute-start) | collective-permute-done | bytes 65568 | tf_op jit(solution)/shard_map/ppermute | solution.py:11
  343.7 5.6 %collective-permute-start.5 = (bf16[128,2,128]{2,1,0:T(2,128)(2,1)S(1)}, bf16[128,2,128]{2,1,0:T(2,128)(2,1)S(1)}, u32[]{:S(2)}, u32[]{:S(2)}) collective-permute-start(bf16[128,2,128]{2,1,0:T(2,128)(2,1)S(1)} %get-tuple-element.5), channel_id=1, source_target_pairs={{0,24},{4,28},{8,32},{12,36},{16,40},{20,44},{24,48},{28,52},{32,5... | collective-permute-start | bytes 196616 | tf_op jit(solution)/shard_map/ppermute | solution.py:11
  349.4 22.5 %collective-permute-start.6 = (bf16[128,2,128]{2,1,0:T(2,128)(2,1)S(1)}, bf16[128,2,128]{2,1,0:T(2,128)(2,1)}, u32[]{:S(2)}, u32[]{:S(2)}) collective-permute-start(bf16[128,2,128]{2,1,0:T(2,128)(2,1)S(1)} %get-tuple-element.4), channel_id=1, source_target_pairs={{0,28},{4,32},{8,36},{12,40},{16,44},{20,48},{24,52},{28,56},{32,6... | collective-permute-start | bytes 196616 | tf_op jit(solution)/shard_map/ppermute | solution.py:11
  372.1 0.8 copy-done.5
  372.9 6.1 %reshape.168 = bf16[1536,1024]{1,0:T(8,128)(2,1)} reshape(bf16[128,1,12,1024]{3,2,1,0:T(8,128)(2,1)} %all-to-all-done.4) | data formatting | bytes 6291456 | tf_op jit(solution)/shard_map/reshape | solution.py:84
  379.0 7.3 %gather_fusion.4 = bf16[1024,1024]{1,0:T(8,128)(2,1)S(1)} fusion(bf16[1536,1024]{1,0:T(8,128)(2,1)} %reshape.168, s32[1024]{0:T(1024)S(1)} %broadcast_clamp_fusion), kind=kCustom, calls=%fused_computation.4 | custom fusion | bytes 4198400 | tf_op jit(solution)/shard_map/gather | solution.py:84
  386.3 2.0 fusion
  388.3 0.7 bitcast_dynamic-update-slice_fusion.2
  389.0 0.7 bitcast_dynamic-update-slice_fusion.1
  389.7 1.5 bitcast_dynamic-update-slice_fusion
  391.2 24.3 %reduce-scatter.2.cloned.1.call-done = bf16[128,256]{1,0:T(8,128)(2,1)} async-done(((bf16[128,1024]{1,0:T(8,128)(2,1)}), bf16[128,256]{1,0:T(8,128)(2,1)}) %reduce-scatter.2.cloned.1.call-update) | async-done | bytes 65552 | tf_op jit(solution)/shard_map/reduce_scatter | solution.py:86
  415.5 1.5 add_convert_fusion
  (57 shorter events, 1.7 us)
Async XLA Ops:
  7.2 243.5 %copy-start = (bf16[8,128,2,128]{3,2,1,0:T(2,128)(2,1)S(1)}, bf16[8,128,2,128]{3,2,1,0:T(2,128)(2,1)}, u32[]{:S(2)}) copy-start(bf16[8,128,2,128]{3,2,1,0:T(2,128)(2,1)} %param.24) | copy-start | bytes 1572868
  7.2 46.6 %all-gather.3.cloned.1.call-start = ((), (), s32[]{:S(2)}) async-start(), calls=%async_computation.7 | async-start | bytes 1310720 | tf_op jit(solution)/shard_map/all_gather | solution.py:35
  13.5 41.9 %all-to-all-start.1 = ((bf16[128,1,8,128]{3,2,1,0:T(8,128)(2,1)}), bf16[128,1,8,128]{3,2,1,0:T(8,128)(2,1)S(1)}, u32[]{:S(2)}, u32[]{:S(2)}) async-start(bf16[128,1,8,128]{3,2,1,0:T(8,128)(2,1)} %bitcast.4), calls=%async_computation.1 | async-start | bytes 524288 | tf_op jit(solution)/shard_map/all_to_all | solution.py:66
  32.6 7.3 %copy-start.4 = (s32[128,8]{0,1:T(8,128)S(1)}, s32[128,8]{0,1:T(8,128)}, u32[]{:S(2)}) copy-start(s32[128,8]{0,1:T(8,128)} %param.22) | copy-start | bytes 12292
  32.7 19.7 %copy-start.1 = (bf16[32,8,128]{2,1,0:T(8,128)(2,1)S(1)}, bf16[32,8,128]{2,1,0:T(8,128)(2,1)}, u32[]{:S(2)}) copy-start(bf16[32,8,128]{2,1,0:T(8,128)(2,1)} %param.20) | copy-start | bytes 196612
  32.7 22.5 %copy-start.3 = (bf16[128,1024]{1,0:T(8,128)(2,1)S(1)}, bf16[128,1024]{1,0:T(8,128)(2,1)}, u32[]{:S(2)}) copy-start(bf16[128,1024]{1,0:T(8,128)(2,1)} %param.15) | copy-start | bytes 786436
  32.7 36.4 %copy-start.6 = (f32[1024]{0:T(1024)S(1)}, f32[1024]{0:T(1024)}, u32[]{:S(2)}) copy-start(f32[1024]{0:T(1024)} %param.18) | copy-start | bytes 12292
  55.4 30.2 %all-to-all-start.3 = ((bf16[128,1,8,128]{3,2,1,0:T(8,128)(2,1)}), bf16[128,1,8,128]{3,2,1,0:T(8,128)(2,1)S(1)}, u32[]{:S(2)}, u32[]{:S(2)}) async-start(bf16[128,1,8,128]{3,2,1,0:T(8,128)(2,1)} %bitcast.16), calls=%async_computation.3 | async-start | bytes 524288 | tf_op jit(solution)/shard_map/all_to_all | solution.py:67
  85.6 14.3 %copy-start.2 = (bf16[32,8,128]{2,1,0:T(8,128)(2,1)S(1)}, bf16[32,8,128]{2,1,0:T(8,128)(2,1)}, u32[]{:S(2)}) copy-start(bf16[32,8,128]{2,1,0:T(8,128)(2,1)} %param.21) | copy-start | bytes 196612
  85.6 110.7 %all-to-all-start.2 = ((bf16[128,1,12,1024]{3,2,1,0:T(8,128)(2,1)}), bf16[128,1,12,1024]{3,2,1,0:T(8,128)(2,1)}, u32[]{:S(2)}, u32[]{:S(2)}) async-start(bf16[128,1,12,1024]{3,2,1,0:T(8,128)(2,1)} %multiply_bitcast_fusion), calls=%async_computation.2 | async-start | bytes 8388608 | tf_op jit(solution)/shard_map/all_to_all | solution.py:76
  196.3 31.2 %all-to-all-start = ((bf16[128,1,8,128]{3,2,1,0:T(8,128)(2,1)}), bf16[128,1,8,128]{3,2,1,0:T(8,128)(2,1)S(1)}, u32[]{:S(2)}, u32[]{:S(2)}) async-start(bf16[128,1,8,128]{3,2,1,0:T(8,128)(2,1)} %bitcast.1), calls=%async_computation | async-start | bytes 524288 | tf_op jit(solution)/shard_map/all_to_all | solution.py:68
  242.6 26.6 %copy-start.7 = (f32[128,8]{0,1:T(8,128)S(1)}, f32[128,8]{0,1:T(8,128)}, u32[]{:S(2)}) copy-start(f32[128,8]{0,1:T(8,128)} %param.23) | copy-start | bytes 12292
  242.6 129.5 %all-to-all-start.4 = ((bf16[128,1,12,1024]{3,2,1,0:T(8,128)(2,1)}), bf16[128,1,12,1024]{3,2,1,0:T(8,128)(2,1)}, u32[]{:S(2)}, u32[]{:S(2)}) async-start(bf16[128,1,12,1024]{3,2,1,0:T(8,128)(2,1)} %copy.82), calls=%async_computation.4 | async-start | bytes 8388608 | tf_op jit(solution)/shard_map/all_to_all | solution.py:83
  250.4 165.1 %reduce-scatter.2.cloned.1.call-start = ((), (), s32[]{:S(2)}) async-start(), calls=%async_computation.6 | async-start | bytes 327680 | tf_op jit(solution)/shard_map/reduce_scatter | solution.py:86
  252.7 91.0 %collective-permute-start = (bf16[128,2,128]{2,1,0:T(2,128)(2,1)S(1)}, bf16[128,2,128]{2,1,0:T(2,128)(2,1)S(1)}, u32[]{:S(2)}, u32[]{:S(2)}) collective-permute-start(bf16[128,2,128]{2,1,0:T(2,128)(2,1)S(1)} %get-tuple-element.10), channel_id=1, source_target_pairs={{0,4},{4,8},{8,12},{12,16},{16,20},{20,24},{24,28},{28,32},{32,36}... | collective-permute-start | bytes 196616 | tf_op jit(solution)/shard_map/ppermute | solution.py:11
  254.7 94.6 %collective-permute-start.1 = (bf16[128,2,128]{2,1,0:T(2,128)(2,1)S(1)}, bf16[128,2,128]{2,1,0:T(2,128)(2,1)S(1)}, u32[]{:S(2)}, u32[]{:S(2)}) collective-permute-start(bf16[128,2,128]{2,1,0:T(2,128)(2,1)S(1)} %get-tuple-element.9), channel_id=1, source_target_pairs={{0,8},{4,12},{8,16},{12,20},{16,24},{20,28},{24,32},{28,36},{32,40... | collective-permute-start | bytes 196616 | tf_op jit(solution)/shard_map/ppermute | solution.py:11
  258.1 113.8 %collective-permute-start.2 = (bf16[128,2,128]{2,1,0:T(2,128)(2,1)S(1)}, bf16[128,2,128]{2,1,0:T(2,128)(2,1)S(1)}, u32[]{:S(2)}, u32[]{:S(2)}) collective-permute-start(bf16[128,2,128]{2,1,0:T(2,128)(2,1)S(1)} %get-tuple-element.8), channel_id=1, source_target_pairs={{0,12},{4,16},{8,20},{12,24},{16,28},{20,32},{24,36},{28,40},{32,4... | collective-permute-start | bytes 196616 | tf_op jit(solution)/shard_map/ppermute | solution.py:11
  262.3 109.7 %collective-permute-start.3 = (bf16[128,2,128]{2,1,0:T(2,128)(2,1)S(1)}, bf16[128,2,128]{2,1,0:T(2,128)(2,1)S(1)}, u32[]{:S(2)}, u32[]{:S(2)}) collective-permute-start(bf16[128,2,128]{2,1,0:T(2,128)(2,1)S(1)} %get-tuple-element.7), channel_id=1, source_target_pairs={{0,16},{4,20},{8,24},{12,28},{16,32},{20,36},{24,40},{28,44},{32,4... | collective-permute-start | bytes 196616 | tf_op jit(solution)/shard_map/ppermute | solution.py:11
  266.9 121.4 %collective-permute-start.4 = (bf16[128,2,128]{2,1,0:T(2,128)(2,1)S(1)}, bf16[128,2,128]{2,1,0:T(2,128)(2,1)S(1)}, u32[]{:S(2)}, u32[]{:S(2)}) collective-permute-start(bf16[128,2,128]{2,1,0:T(2,128)(2,1)S(1)} %get-tuple-element.6), channel_id=1, source_target_pairs={{0,20},{4,24},{8,28},{12,32},{16,36},{20,40},{24,44},{28,48},{32,5... | collective-permute-start | bytes 196616 | tf_op jit(solution)/shard_map/ppermute | solution.py:11
  343.7 45.3 %collective-permute-start.5 = (bf16[128,2,128]{2,1,0:T(2,128)(2,1)S(1)}, bf16[128,2,128]{2,1,0:T(2,128)(2,1)S(1)}, u32[]{:S(2)}, u32[]{:S(2)}) collective-permute-start(bf16[128,2,128]{2,1,0:T(2,128)(2,1)S(1)} %get-tuple-element.5), channel_id=1, source_target_pairs={{0,24},{4,28},{8,32},{12,36},{16,40},{20,44},{24,48},{28,52},{32,5... | collective-permute-start | bytes 196616 | tf_op jit(solution)/shard_map/ppermute | solution.py:11
  349.4 40.3 %collective-permute-start.6 = (bf16[128,2,128]{2,1,0:T(2,128)(2,1)S(1)}, bf16[128,2,128]{2,1,0:T(2,128)(2,1)}, u32[]{:S(2)}, u32[]{:S(2)}) collective-permute-start(bf16[128,2,128]{2,1,0:T(2,128)(2,1)S(1)} %get-tuple-element.4), channel_id=1, source_target_pairs={{0,28},{4,32},{8,36},{12,40},{16,44},{20,48},{24,52},{28,56},{32,6... | collective-permute-start | bytes 196616 | tf_op jit(solution)/shard_map/ppermute | solution.py:11
  372.1 0.8 copy-start.5
Sparse Core Ops, SparseCore 0:
  10.7 33.8 all-gather.2
  388.4 26.9 reduce-scatter.1
